TPU v7x, 128 devices: a whole 4x4x4 slice. The times are simulated.
128 devices in a mesh: gx: 16 (over x, y), gy: 8 (over z, core).
Axes of the slice: x: 4, y: 4, z: 4, core: 2. Of those that a mesh axis runs over, the one named last changes fastest.
Arguments:
- plume_field: bfloat16 [2, 20, 128, 128, 16, 128], P(None, None, 'gx', 'gy'), may hold values from -6 to 6
- mode_weights: bfloat16 [24, 20, 20, 16, 2, 288], P('gy', None, None, 'gx'), may hold values from -1 to 1
Outputs:
- spectral_mix: float32 [2, 24, 20, 16, 2, 288], P(None, 'gy', None, 'gx')
All inputs are finite; a program needn't handle non-finite values.
Results may differ from a plain program's by a relative error of at most 0.003.
Values sent between devices are 32-bit elements; how exact they have to be, the bound alone decides.
A program may use at most 192 MiB of HBM per device.

v0:
```python
import math

import jax
import jax.numpy as jnp
from jax import lax
from jax.sharding import PartitionSpec as P

GRID_X = 128
GRID_Y = 128
GRID_Z = 128
STEPS_T = 16
MODES_X = 24
MODES_Y = 24
MODES_Z = 24
MODES_T = 8
HALF_Z = 12


def kept_modes(kept_count, axis_length):
    position = jnp.arange(kept_count, dtype=jnp.int32)
    return jnp.where(position < kept_count // 2, position, axis_length - kept_count + position)


def plane_table():
    moments = jnp.arange(STEPS_T, dtype=jnp.int32)
    depths = jnp.arange(GRID_Z, dtype=jnp.int32)
    time_freq = jnp.arange(MODES_T, dtype=jnp.int32)
    depth_freq = kept_modes(MODES_Z, GRID_Z).reshape(2, HALF_Z)
    phase_index = (
        time_freq[None, None, :, None, None]
        * moments[:, None, None, None, None]
        * (GRID_Z // STEPS_T)
        + depth_freq[None, None, None, :, :] * depths[None, :, None, None, None]
    ) % GRID_Z
    phases = 2.0 * math.pi / GRID_Z * phase_index.astype(jnp.float32)
    factor = 1.0 / math.sqrt(STEPS_T * GRID_Z)
    twiddle = jnp.stack([factor * jnp.cos(phases), -factor * jnp.sin(phases)], axis=4)
    return twiddle.reshape(STEPS_T * GRID_Z, 2 * MODES_T * MODES_Z).astype(jnp.bfloat16)


def line_parts(kept_count, axis_length, positions):
    frequency = kept_modes(kept_count, axis_length)
    phase_index = positions[:, None] * frequency[None, :] % axis_length
    phases = 2.0 * math.pi / axis_length * phase_index.astype(jnp.float32)
    factor = 1.0 / math.sqrt(axis_length)
    return (factor * jnp.cos(phases), factor * jnp.sin(phases))


def across_x(modes_in, cosines, sines):
    highest = lax.Precision.HIGHEST
    real_part = modes_in[:, 0]
    imag_part = modes_in[:, 1]
    out_real = jnp.einsum("xk,gjxm->gjkm", cosines, real_part, precision=highest) + jnp.einsum(
        "xk,gjxm->gjkm", sines, imag_part, precision=highest
    )
    out_imag = jnp.einsum("xk,gjxm->gjkm", cosines, imag_part, precision=highest) - jnp.einsum(
        "xk,gjxm->gjkm", sines, real_part, precision=highest
    )
    return jnp.stack([out_real, out_imag], axis=1)


def across_y(modes_in, cosines, sines):
    highest = lax.Precision.HIGHEST
    real_part = modes_in[:, 0]
    imag_part = modes_in[:, 1]
    out_real = jnp.dot(real_part, cosines, precision=highest) + jnp.dot(
        imag_part, sines, precision=highest
    )
    out_imag = jnp.dot(imag_part, cosines, precision=highest) - jnp.dot(
        real_part, sines, precision=highest
    )
    stacked = jnp.stack([out_real, out_imag], axis=1)
    groups_here, _, half_count, mode_count, samples, channels, kept_count = stacked.shape
    stacked = jnp.transpose(stacked, (3, 4, 5, 0, 1, 2, 6))
    return stacked.reshape(mode_count, samples, channels, groups_here, 2, half_count * kept_count)


def mix_modes(modes, mode_weights):
    real_part = modes[:, :, :, None, :, 0]
    imag_part = modes[:, :, :, None, :, 1]
    weight_re = mode_weights[:, None, :, :, :, 0].astype(jnp.float32)
    weight_im = mode_weights[:, None, :, :, :, 1].astype(jnp.float32)
    mixed_re = jnp.sum(real_part * weight_re - imag_part * weight_im, axis=2)
    mixed_im = jnp.sum(real_part * weight_im + imag_part * weight_re, axis=2)
    mixed = jnp.stack([mixed_re, mixed_im], axis=4)
    return jnp.swapaxes(mixed, 0, 1)


def local(plume_field, mode_weights):
    samples, channels, rows_first, rows_second = plume_field.shape[:4]
    groups_here = mode_weights.shape[3]
    twiddle = plane_table()
    leading = jnp.moveaxis(plume_field, 2, 0).reshape(-1, STEPS_T * GRID_Z)
    spectrum = lax.dot_general(
        twiddle, leading, (((0,), (1,)), ((), ())), preferred_element_type=jnp.float32
    )
    inner = samples * channels * rows_second
    moved = lax.all_to_all(spectrum, "gx", split_axis=0, concat_axis=1, tiled=True)
    moved = moved.reshape(groups_here, 2, HALF_Z, GRID_X, inner)
    cosines, sines = line_parts(MODES_X, GRID_X, jnp.arange(GRID_X, dtype=jnp.int32))
    after_first = across_x(moved, cosines, sines)
    after_first = after_first.reshape(
        groups_here, 2, HALF_Z, MODES_X, samples, channels, rows_second
    )
    first_column = lax.axis_index("gy") * rows_second
    cosines_y, sines_y = line_parts(
        MODES_Y, GRID_Y, first_column + jnp.arange(rows_second, dtype=jnp.int32)
    )
    after_second = lax.psum_scatter(
        across_y(after_first, cosines_y, sines_y), "gy", scatter_dimension=0, tiled=True
    )
    return mix_modes(after_second, mode_weights)


def solution(mesh):
    return jax.shard_map(
        local,
        mesh=mesh,
        in_specs=(P(None, None, "gx", "gy", None, None), P("gy", None, None, "gx", None, None)),
        out_specs=P(None, "gy", None, "gx", None, None),
        check_vma=False,
    )
```

profile of v0, /device:TPU:1, one launch (start us, length us, event | category | flops | bytes accessed | tf_op | source)
XLA Modules:
  0.0 435.8 jit_solution(7727469673252502097)
XLA Ops:
  6.6 6.7 %multiply_convert_fusion.1 = (bf16[16,128,8,2,1,12]{1,0,5,4,3,2:T(8,128)(2,1)S(1)}, bf16[16,128,8,2,1,12]{1,0,5,4,3,2:T(8,128)(2,1)S(1)}) fusion(s32[128,2,12]{0,2,1:T(8,128)S(1)} %iota_multiply_fusion, s32[16,8]{0,1:T(8,128)S(1)} %multiply_multiply_fusion), kind=kLoop, calls=%fused_computation.22 | loop fusion | flops 7077888 | bytes 1585664 | tf_op jit(solution)/shard_map/convert.2
  13.4 0.4 copy.59
  13.9 19.0 %copy.32 = bf16[8,2,20,16,16,128]{5,4,3,2,1,0:T(8,128)(2,1)} copy(bf16[8,2,20,16,16,128]{5,4,3,0,2,1:T(8,128)(2,1)} %bitcast.101) | data formatting | bytes 41943040 | tf_op jit(solution)/shard_map/transpose | solution.py:93
  32.8 31.3 %reshape.226 = bf16[5120,2048,1]{1,0,2:T(8,128)(2,1)} reshape(bf16[8,2,20,16,16,128]{5,4,3,2,1,0:T(8,128)(2,1)} %copy.32) | data formatting | bytes 41943040 | tf_op jit(solution)/shard_map/reshape | solution.py:93
  64.1 14.4 %fusion.89 = f32[16,24,5120]{2,1,0:T(8,128)} fusion(bf16[16,24,2048]{2,1,0:T(8,128)(2,1)S(1)} %bitcast.103, bf16[5120,2048,1]{1,0,2:T(8,128)(2,1)} %reshape.226), kind=kOutput, calls=%fused_computation.121 | convolution fusion | flops 8053063680 | bytes 30408704 | tf_op jit(solution)/shard_map/dot_general | solution.py:94
  78.5 7.7 %all-to-all-start = ((f32[16,24,5120]{2,1,0:T(8,128)}), f32[16,24,5120]{2,1,0:T(8,128)}, u32[]{:S(2)}, u32[]{:S(2)}) async-start(f32[16,24,5120]{2,1,0:T(8,128)} %fusion.89), calls=%async_computation | async-start | bytes 15728640 | tf_op jit(solution)/shard_map/all_to_all | solution.py:98
  86.3 0.3 all-reduce.3.cloned.1.call-start
  86.6 0.6 dynamic-slice
  87.9 133.6 %all-to-all-done = f32[16,24,5120]{2,1,0:T(8,128)} async-done(((f32[16,24,5120]{2,1,0:T(8,128)}), f32[16,24,5120]{2,1,0:T(8,128)}, u32[]{:S(2)}, u32[]{:S(2)}) %all-to-all-start) | async-done | bytes 7864352 | tf_op jit(solution)/shard_map/all_to_all | solution.py:98
  221.5 10.9 %copy.33 = f32[24,16,5120]{2,1,0:T(8,128)} copy(f32[24,16,5120]{2,0,1:T(8,128)} %bitcast.3) | data formatting | bytes 15728640 | tf_op jit(solution)/shard_map/all_to_all | solution.py:98
  232.4 9.7 %reshape.218 = f32[1,2,12,128,640]{4,3,2,1,0:T(8,128)} reshape(f32[24,16,5120]{2,1,0:T(8,128)} %copy.33) | data formatting | bytes 15728640 | tf_op jit(solution)/shard_map/reshape | solution.py:99
  242.1 4.5 %fusion.1 = f32[12,640,24]{1,2,0:T(8,128)S(1)} fusion(f32[1,2,12,128,640]{4,3,2,1,0:T(8,128)} %reshape.218, s32[24]{0:T(128)S(1)} %compare_select_fusion.1), kind=kOutput, calls=%fused_computation.6 | convolution fusion | flops 283161600 | bytes 4669536 | tf_op jit(solution)/shard_map/xk,gjxm->gjkm/dot_general | solution.py:53
  246.6 4.3 fusion
  250.9 2.2 fusion.8
  253.2 2.6 copy.34
  255.8 4.4 fusion.10
  260.2 2.7 copy.35
  262.8 11.9 %fusion.30 = f32[12,24,2,20,24]{4,1,3,2,0:T(8,128)S(1)} fusion(f32[12,24,2,20,16]{1,4,3,2,0:T(8,128)} %bitcast.97, s32[24]{0:T(128)S(1)} %compare_select_fusion.1, s32[16]{0:T(128)S(1)} %iota_add_fusion), kind=kOutput, calls=%fused_computation.62 | convolution fusion | flops 53089920 | bytes 1843360 | tf_op jit(solution)/shard_map/dot_general | solution.py:66
  274.7 9.6 %fusion.28 = f32[12,24,2,20,24]{4,1,3,2,0:T(8,128)S(1)} fusion(f32[12,24,2,20,16]{1,4,3,2,0:T(8,128)S(1)} %bitcast.99, s32[24]{0:T(128)S(1)} %compare_select_fusion.1, s32[16]{0:T(128)S(1)} %iota_add_fusion), kind=kOutput, calls=%fused_computation.60 | convolution fusion | flops 53089920 | bytes 1843360 | tf_op jit(solution)/shard_map/dot_general | solution.py:69
  284.3 10.1 %add_bitcast_fusion = f32[1,1,12,24,2,20,24]{6,3,5,4,2,1,0:T(8,128)S(1)} fusion(f32[12,24,2,20,24]{4,1,3,2,0:T(8,128)S(1)} %fusion.30, f32[12,24,2,20,16]{1,4,3,2,0:T(8,128)S(1)} %bitcast.100, s32[24]{0:T(128)S(1)} %compare_select_fusion.1, s32[16]{0:T(128)S(1)} %iota_add_fusion), kind=kOutput, calls=%fused_computation.2 | convolution fusion | flops 53366400 | bytes 2949280 | tf_op jit(solution)/shard_map/dot_general | solution.py:66
  294.4 11.8 %subtract_bitcast_fusion = f32[1,1,12,24,2,20,24]{6,3,5,4,2,1,0:T(8,128)} fusion(f32[12,24,2,20,24]{4,1,3,2,0:T(8,128)S(1)} %fusion.28, f32[12,24,2,20,16]{1,4,3,2,0:T(8,128)S(1)} %bitcast.98, s32[24]{0:T(128)S(1)} %compare_select_fusion.1, s32[16]{0:T(128)S(1)} %iota_add_fusion), kind=kOutput, calls=%fused_computation.1 | convolution fusion | flops 53366400 | bytes 2949280 | tf_op jit(solution)/shard_map/dot_general | solution.py:69
  306.2 8.3 %maximum_bitcast_fusion = f32[24,2,20,1,2,12,24]{6,0,2,1,5,4,3:T(8,128)} fusion(f32[1,1,12,24,2,20,24]{6,3,5,4,2,1,0:T(8,128)} %subtract_bitcast_fusion, f32[1,1,12,24,2,20,24]{6,3,5,4,2,1,0:T(8,128)S(1)} %add_bitcast_fusion), kind=kLoop, calls=%fused_computation | loop fusion | flops 552960 | bytes 4423680 | tf_op jit(solution)/shard_map/transpose | solution.py:74
  314.5 16.9 %copy.45 = f32[24,2,20,1,2,12,24]{6,5,4,2,1,0,3:T(8,128)} copy(f32[24,2,20,1,2,12,24]{6,0,2,1,5,4,3:T(8,128)} %maximum_bitcast_fusion) | data formatting | bytes 4423680 | tf_op jit(solution)/shard_map/reshape | solution.py:75
  331.4 13.6 %reshape.232 = f32[24,2,20,1,2,288]{5,4,3,2,1,0:T(2,128)} reshape(f32[24,2,20,1,2,12,24]{6,5,4,2,1,0,3:T(8,128)} %copy.45) | data formatting | bytes 4423680 | tf_op jit(solution)/shard_map/reshape | solution.py:75
  345.0 1.5 copy-done.3
  346.5 2.5 fusion.88
  349.1 1.8 fusion.11
  350.9 68.0 %all-reduce.3.cloned.1.call-done = f32[24,2,20,1,2,288]{5,4,3,2,1,0:T(2,128)} async-done(((f32[24,2,20,1,2,288]{5,4,3,2,1,0:T(2,128)}), f32[24,2,20,1,2,288]{5,4,3,2,1,0:T(2,128)}) %all-reduce.3.cloned.1.call-update) | async-done | bytes 2211856
  418.9 1.4 constant_dynamic-slice_fusion
  420.3 0.2 copy_bitcast_fusion.3
  420.5 7.1 %subtract_reduce_fusion = (f32[3,2,20,288]{3,1,2,0:T(2,128)S(1)}, f32[3,2,20,288]{3,1,2,0:T(2,128)S(1)}) fusion(f32[3,20,20,288]{3,2,1,0:T(8,128)S(1)} %get-tuple-element.13, f32[3,2,20,288]{3,1,2,0:T(2,128)S(1)} %get-tuple-element.15, f32[3,20,20,288]{3,2,1,0:T(8,128)} %get-tuple-element.14, f32[3,2,20,288]{3,1,2,0:T(2,128)S(1)} %get-tuple-element.16), kind=kLoop, calls=%fused_computation.10 | loop fusion | flops 5460480 | bytes 3317760 | tf_op jit(solution)/shard_map/reduce_sum | solution.py:83
  427.8 0.9 copy.42
  (17 shorter events, 0.5 us)
Async XLA Ops:
  78.5 8.1 %copy-start.4 = (u32[128]{0:T(128)S(1)}, u32[128]{0:T(128)}, u32[]{:S(2)}) copy-start(u32[128]{0:T(128)} %constant.63) | copy-start | bytes 1540
  78.5 143.0 %all-to-all-start = ((f32[16,24,5120]{2,1,0:T(8,128)}), f32[16,24,5120]{2,1,0:T(8,128)}, u32[]{:S(2)}, u32[]{:S(2)}) async-start(f32[16,24,5120]{2,1,0:T(8,128)} %fusion.89), calls=%async_computation | async-start | bytes 15728640 | tf_op jit(solution)/shard_map/all_to_all | solution.py:98
  86.3 332.6 %all-reduce.3.cloned.1.call-start = ((), (), s32[]{:S(2)}) async-start(), calls=%async_computation.1 | async-start | bytes 5898240
  242.1 8.8 %copy-start = (f32[1,2,12,128,640]{4,3,2,1,0:T(8,128)S(1)}, f32[1,2,12,128,640]{4,3,2,1,0:T(8,128)}, u32[]{:S(2)}) copy-start(f32[1,2,12,128,640]{4,3,2,1,0:T(8,128)} %reshape.218) | copy-start | bytes 23592964
  262.8 11.9 %copy-start.2 = (f32[1,12,24,640]{2,3,1,0:T(8,128)S(1)}, f32[1,12,24,640]{2,3,1,0:T(8,128)}, u32[]{:S(2)}) copy-start(f32[1,12,24,640]{2,3,1,0:T(8,128)} %copy.35) | copy-start | bytes 2211844
  284.3 10.1 %copy-start.1 = (f32[1,12,24,640]{2,3,1,0:T(8,128)S(1)}, f32[1,12,24,640]{2,3,1,0:T(8,128)}, u32[]{:S(2)}) copy-start(f32[1,12,24,640]{2,3,1,0:T(8,128)} %copy.34) | copy-start | bytes 2211844
  345.0 1.5 copy-start.3
Sparse Core Ops, SparseCore 0:
  345.2 73.6 all-reduce.2
where the time goes:
time: 444 us; the launch traced here: 436 us
  waiting for transfers between devices  202 us (45%)
  local copies, waits for them, and re-layouts  114 us (26%)
  matrix products  73.1 us (16%)
  other arithmetic  24.3 us (5%)
  between operations  14.5 us (3%)
  starting transfers between devices  8.08 us (2%)
    all_to_all x1, waiting for transfers between devices, local(): lax.all_to_all(spectrum, 'gx', split_axis=0, concat_axis=1, tiled=True)  134 us
    unnamed x2, waiting for transfers between devices  68 us
    reshape x1, local copies, waits for them, and re-layouts, local(): leading = jnp.moveaxis(plume_field, 2, 0).reshape(-1, STEPS_T * GRID_Z)  31.3 us
    reshape x2, local copies, waits for them, and re-layouts, across_y(): stacked.reshape(mode_count, samples, channels, groups_here, 2, half_count...  30.5 us
    transpose x1, local copies, waits for them, and re-layouts, local(): leading = jnp.moveaxis(plume_field, 2, 0).reshape(-1, STEPS_T * GRID_Z)  19 us
    dot_general x1, matrix products, local(): lax.dot_general(twiddle, leading, (((0,), (1,)), ((), ())), preferred_ele...  14.4 us
    dot_general x1, matrix products, across_y(): jnp.dot(real_part, cosines, precision=highest)  11.9 us
    dot_general x1, matrix products, across_y(): jnp.dot(real_part, sines, precision=highest)  11.8 us
  transfers between devices with their start and end apart: 2, of which 2 were waited for; matrix products, arithmetic and copies ran while one was open for 1% of the time, Pallas kernels for 0%

commit v1 on v0

v1 whole, which is shorter than its diff:
```python
import math

import jax
import jax.numpy as jnp
from jax import lax
from jax.sharding import PartitionSpec as P

GRID_X = 128
GRID_Y = 128
GRID_Z = 128
STEPS_T = 16
MODES_X = 24
MODES_Y = 24
MODES_Z = 24
MODES_T = 8
HALF_Z = 12


def kept_modes(kept_count, axis_length):
    position = jnp.arange(kept_count, dtype=jnp.int32)
    return jnp.where(position < kept_count // 2, position, axis_length - kept_count + position)


def plane_table():
    moments = jnp.arange(STEPS_T, dtype=jnp.int32)
    depths = jnp.arange(GRID_Z, dtype=jnp.int32)
    time_freq = jnp.arange(MODES_T, dtype=jnp.int32)
    depth_freq = kept_modes(MODES_Z, GRID_Z).reshape(2, HALF_Z)
    phase_index = (
        time_freq[None, None, :, None, None]
        * moments[:, None, None, None, None]
        * (GRID_Z // STEPS_T)
        + depth_freq[None, None, None, :, :] * depths[None, :, None, None, None]
    ) % GRID_Z
    phases = 2.0 * math.pi / GRID_Z * phase_index.astype(jnp.float32)
    factor = 1.0 / math.sqrt(STEPS_T * GRID_Z)
    twiddle = jnp.stack([factor * jnp.cos(phases), -factor * jnp.sin(phases)], axis=4)
    return twiddle.reshape(STEPS_T, GRID_Z, 2 * MODES_T * MODES_Z).astype(jnp.bfloat16)


def line_matrix(kept_count, axis_length):
    frequency = kept_modes(kept_count, axis_length)
    positions = jnp.arange(axis_length, dtype=jnp.int32)
    phase_index = frequency[:, None] * positions[None, :] % axis_length
    phases = 2.0 * math.pi / axis_length * phase_index.astype(jnp.float32)
    factor = 1.0 / math.sqrt(axis_length)
    cosines = factor * jnp.cos(phases)
    sines = factor * jnp.sin(phases)
    upper = jnp.stack([cosines, sines], axis=1)
    lower = jnp.stack([-sines, cosines], axis=1)
    return jnp.stack([upper, lower], axis=0)


def local(plume_field, mode_weights):
    highest = lax.Precision.HIGHEST
    samples, channels, rows_x, rows_y = plume_field.shape[:4]
    parts_x = GRID_X // rows_x
    parts_y = GRID_Y // rows_y
    groups = 2 * MODES_T
    per_group = 2 * HALF_Z
    kept_here = MODES_X // parts_y

    twiddle = plane_table()
    spectrum = lax.dot_general(
        twiddle, plume_field, (((0, 1), (4, 5)), ((), ())), preferred_element_type=jnp.float32
    )
    spectrum = spectrum.reshape(groups, per_group, samples * channels * rows_x * rows_y)
    moved = lax.all_to_all(spectrum, "gx", 0, 0, tiled=False)
    moved = moved.reshape(parts_x, 2, HALF_Z, samples, channels, rows_x, rows_y)

    first = line_matrix(MODES_X, GRID_X).reshape(2, parts_y, kept_here, 2, parts_x, rows_x)
    after_x = jnp.einsum("sKqrip,irjbcpy->Kysqjbc", first, moved, precision=highest)
    after_x = after_x.reshape(parts_y, rows_y, -1)
    gathered = lax.all_to_all(after_x, "gy", 0, 0, tiled=False)
    gathered = gathered.reshape(GRID_Y, 2, kept_here, HALF_Z, samples, channels)

    second = line_matrix(MODES_Y, GRID_Y)
    after_y = jnp.einsum("tlsy,yskjbc->kbctjl", second, gathered, precision=highest)
    after_y = after_y.reshape(kept_here, samples, channels, 2, HALF_Z * MODES_Y)

    real_part = after_y[:, :, :, None, 0]
    imag_part = after_y[:, :, :, None, 1]
    weight_re = mode_weights[:, None, :, :, 0, 0].astype(jnp.float32)
    weight_im = mode_weights[:, None, :, :, 0, 1].astype(jnp.float32)
    mixed_re = jnp.sum(real_part * weight_re - imag_part * weight_im, axis=2)
    mixed_im = jnp.sum(real_part * weight_im + imag_part * weight_re, axis=2)
    mixed = jnp.stack([mixed_re, mixed_im], axis=3)[:, :, :, None]
    return jnp.swapaxes(mixed, 0, 1)


def solution(mesh):
    return jax.shard_map(
        local,
        mesh=mesh,
        in_specs=(P(None, None, "gx", "gy", None, None), P("gy", None, None, "gx", None, None)),
        out_specs=P(None, "gy", None, "gx", None, None),
        check_vma=False,
    )
```

time: 444 us -> 409 us (0.921)
  waiting for transfers between devices: 202 us -> 150 us
  local copies, waits for them, and re-layouts: 114 us -> 152 us
  between operations: 14.5 us -> 0.14 us
  other arithmetic: 24.3 us -> 16.6 us
  starting transfers between devices: 8.08 us -> 15.6 us
    unnamed x2 -> x0, waiting for transfers between devices: 68 us -> none
    reshape x4 -> x5, local copies, waits for them, and re-layouts: 71.5 us -> 137 us  [the longest x2 101 us: local(): moved = moved.reshape(parts_x, 2, HALF_Z, samples, channels, rows_x, rows_y)]
    all_to_all x1 -> x2, waiting for transfers between devices: 134 us -> 150 us  [the longest x1 135 us: local(): moved = lax.all_to_all(spectrum, 'gx', 0, 0, tiled=False)]
    all_to_all x1 -> x0, local copies, waits for them, and re-layouts: 10.9 us -> none  [local(): lax.all_to_all(spectrum, 'gx', split_axis=0, concat_axis=1, tiled=True)]
    transpose x2 -> x1, other arithmetic: 8.47 us -> 0.17 us  [local(): return jnp.swapaxes(mixed, 0, 1)]
    transpose x2 -> x3, local copies, waits for them, and re-layouts: 19.9 us -> 11.7 us  [the longest x1 8.59 us: local(): jnp.einsum('sKqrip,irjbcpy->Kysqjbc', first, moved, precision=highest)]
    all_to_all x1 -> x2, starting transfers between devices: 7.74 us -> 15.6 us  [the longest x1 7.94 us: local(): gathered = lax.all_to_all(after_x, 'gy', 0, 0, tiled=False)]
    dot_general x9 -> x3, matrix products: 73.1 us -> 69.5 us  [the longest x1 35.9 us: local(): jnp.einsum('sKqrip,irjbcpy->Kysqjbc', first, moved, precision=highest)]
where the time goes in v1:
time: 409 us; the launch traced here: 404 us
  local copies, waits for them, and re-layouts  152 us (37%)
  waiting for transfers between devices  150 us (37%)
  matrix products  69.5 us (17%)
  other arithmetic  16.6 us (4%)
  starting transfers between devices  15.6 us (4%)
    all_to_all x1, waiting for transfers between devices, local(): moved = lax.all_to_all(spectrum, 'gx', 0, 0, tiled=False)  135 us
    reshape x2, local copies, waits for them, and re-layouts, local(): moved = moved.reshape(parts_x, 2, HALF_Z, samples, channels, rows_x, rows_y)  101 us
    dot_general x1, matrix products, local(): jnp.einsum('sKqrip,irjbcpy->Kysqjbc', first, moved, precision=highest)  35.9 us
    dot_general x1, matrix products, local(): jnp.einsum('tlsy,yskjbc->kbctjl', second, gathered, precision=highest)  18.7 us
    reshape x1, local copies, waits for them, and re-layouts, local(): gathered = gathered.reshape(GRID_Y, 2, kept_here, HALF_Z, samples, channels)  17.7 us
    reshape x1, local copies, waits for them, and re-layouts, local(): after_x = after_x.reshape(parts_y, rows_y, -1)  15.9 us
    all_to_all x1, waiting for transfers between devices, local(): gathered = lax.all_to_all(after_x, 'gy', 0, 0, tiled=False)  15.5 us
    dot_general x1, matrix products, local(): lax.dot_general(twiddle, plume_field, (((0, 1), (4, 5)), ((), ())), prefe...  14.8 us
  transfers between devices with their start and end apart: 2, of which 2 were waited for; matrix products, arithmetic and copies ran while one was open for 1% of the time, Pallas kernels for 0%

profile of v1, /device:TPU:1, one launch (start us, length us, event | category | flops | bytes accessed | tf_op | source)
XLA Modules:
  0.0 403.8 jit_solution(13047111962114055903)
XLA Ops:
  0.0 0.1 iota_multiply_fusion
  0.1 6.7 %multiply_convert_fusion.1 = (bf16[16,128,8,2,1,12]{1,0,5,4,3,2:T(8,128)(2,1)S(1)}, bf16[16,128,8,2,1,12]{1,0,5,4,3,2:T(8,128)(2,1)S(1)}) fusion(s32[128,2,12]{0,2,1:T(8,128)S(1)} %iota_multiply_fusion, s32[16,8]{0,1:T(8,128)S(1)} %multiply_multiply_fusion), kind=kLoop, calls=%fused_computation.20 | loop fusion | flops 7077888 | bytes 1585664 | tf_op jit(solution)/shard_map/convert.2
  6.7 0.2 pad_maximum_fusion
  6.9 14.8 %fusion.5 = f32[16,24,5120]{2,1,0:T(8,128)} fusion(bf16[5120,16,128]{2,1,0:T(8,128)(2,1)} %bitcast.73, bf16[16,24,16,128]{3,2,1,0:T(8,128)(2,1)S(1)} %bitcast.70), kind=kOutput, calls=%fused_computation.5 | convolution fusion | flops 8053063680 | bytes 30408704 | tf_op jit(solution)/shard_map/dot_general | solution.py:64
  21.7 7.6 %all-to-all-start = ((f32[16,24,5120]{2,1,0:T(8,128)}), f32[16,24,5120]{2,1,0:T(8,128)}, u32[]{:S(2)}, u32[]{:S(2)}) async-start(f32[16,24,5120]{2,1,0:T(8,128)} %fusion.5), calls=%async_computation | async-start | bytes 15728640 | tf_op jit(solution)/shard_map/all_to_all | solution.py:68
  29.4 0.5 sine_multiply_fusion
  29.9 134.7 %all-to-all-done = f32[16,24,5120]{2,1,0:T(8,128)} async-done(((f32[16,24,5120]{2,1,0:T(8,128)}), f32[16,24,5120]{2,1,0:T(8,128)}, u32[]{:S(2)}, u32[]{:S(2)}) %all-to-all-start) | async-done | bytes 7864352 | tf_op jit(solution)/shard_map/all_to_all | solution.py:68
  164.6 31.1 %reshape.330 = f32[16,2,12,2,20,8,16]{6,5,4,3,2,1,0:T(8,128)} reshape(f32[16,24,5120]{2,1,0:T(8,128)} %all-to-all-done) | data formatting | bytes 15728640 | tf_op jit(solution)/shard_map/reshape | solution.py:69
  195.6 69.9 %copy.31 = f32[16,2,12,2,20,8,16,1,1]{4,0,1,5,8,7,6,3,2:T(8,128)} copy(f32[16,2,12,2,20,8,16,1,1]{6,5,4,3,2,1,0,8,7:T(8,128)} %bitcast.68) | data formatting | bytes 15728640 | tf_op jit(solution)/shard_map/reshape | solution.py:69
  265.5 35.9 %convolution_bitcast_fusion = f32[8,16,2,3,12,2,20]{6,0,3,2,1,5,4:T(8,128)S(1)} fusion(f32[16,2,12,2,20,8,16,1,1]{4,0,1,5,8,7,6,3,2:T(8,128)} %copy.31, f32[2,8,3,2,16,8,1,1,1]{4,1,3,5,2,0,8,7,6:T(8,128)S(1)} %maximum_bitcast_fusion.9), kind=kOutput, calls=%fused_computation.8 | convolution fusion | flops 1132462080 | bytes 9388032 | tf_op jit(solution)/shard_map/sKqrip,irjbcpy->Kysqjbc/dot_general | solution.py:72
  301.5 8.6 %copy.22 = f32[8,16,2,3,12,2,20]{6,5,4,3,2,1,0:T(2,128)} copy(f32[8,16,2,3,12,2,20]{6,0,3,2,1,5,4:T(8,128)S(1)} %convolution_bitcast_fusion) | data formatting | bytes 2949120 | tf_op jit(solution)/shard_map/sKqrip,irjbcpy->Kysqjbc/transpose | solution.py:72
  310.1 15.9 %reshape.331 = f32[8,16,2880]{2,1,0:T(8,128)} reshape(f32[8,16,2,3,12,2,20]{6,5,4,3,2,1,0:T(2,128)} %copy.22) | data formatting | bytes 2949120 | tf_op jit(solution)/shard_map/reshape | solution.py:73
  326.0 0.0 copy-start
  326.0 7.9 %all-to-all-start.1 = ((f32[8,16,2880]{2,1,0:T(8,128)}), f32[8,16,2880]{2,1,0:T(8,128)}, u32[]{:S(2)}, u32[]{:S(2)}) async-start(f32[8,16,2880]{2,1,0:T(8,128)} %reshape.331), calls=%async_computation.1 | async-start | bytes 3014656 | tf_op jit(solution)/shard_map/all_to_all | solution.py:74
  333.9 0.1 sine_multiply_fusion.1
  334.1 0.0 copy-done
  334.1 2.5 fusion.38
  336.6 1.8 fusion.15
  338.4 15.5 %all-to-all-done.1 = f32[8,16,2880]{2,1,0:T(8,128)} async-done(((f32[8,16,2880]{2,1,0:T(8,128)}), f32[8,16,2880]{2,1,0:T(8,128)}, u32[]{:S(2)}, u32[]{:S(2)}) %all-to-all-start.1) | async-done | bytes 1474592 | tf_op jit(solution)/shard_map/all_to_all | solution.py:74
  353.9 17.7 %reshape.332 = f32[128,2,3,12,2,20]{5,4,3,2,1,0:T(2,128)} reshape(f32[8,16,2880]{2,1,0:T(8,128)} %all-to-all-done.1) | data formatting | bytes 2949120 | tf_op jit(solution)/shard_map/reshape | solution.py:75
  371.6 18.7 %fusion.12 = f32[3,2,20,2,12,24]{5,2,3,1,4,0:T(8,128)S(1)} fusion(f32[128,2,3,12,2,20,1]{5,4,3,2,1,0,6:T(2,128)} %bitcast.69, f32[1,24,2,128]{3,1,2,0:T(8,128)S(1)} %get-tuple-element.14, f32[1,24,2,128]{3,1,2,0:T(8,128)S(1)} %get-tuple-element.13), kind=kOutput, calls=%fused_computation.21 | convolution fusion | flops 212348928 | bytes 1800192 | tf_op jit(solution)/shard_map/tlsy,yskjbc->kbctjl/dot_general | solution.py:78
  390.4 2.2 copy.24
  392.6 2.6 reshape.333
  395.2 0.3 fusion.39
  395.5 0.2 copy_bitcast_fusion.2
  395.7 7.1 %subtract_reduce_fusion = (f32[3,2,20,288]{3,1,2,0:T(2,128)S(1)}, f32[3,2,20,288]{3,1,2,0:T(2,128)S(1)}) fusion(f32[3,20,20,288]{3,2,1,0:T(8,128)S(1)} %get-tuple-element.21, f32[3,2,20,288]{3,1,2,0:T(2,128)S(1)} %get-tuple-element.23, f32[3,20,20,288]{3,2,1,0:T(8,128)} %get-tuple-element.22, f32[3,2,20,288]{3,1,2,0:T(2,128)S(1)} %get-tuple-element.24), kind=kLoop, calls=%fused_computation.7 | loop fusion | flops 5460480 | bytes 3317760 | tf_op jit(solution)/shard_map/reduce_sum | solution.py:85
  402.7 0.2 maximum_bitcast_fusion.2
  402.9 0.9 copy.29
  (7 shorter events, 0.1 us)
Async XLA Ops:
  21.7 142.9 %all-to-all-start = ((f32[16,24,5120]{2,1,0:T(8,128)}), f32[16,24,5120]{2,1,0:T(8,128)}, u32[]{:S(2)}, u32[]{:S(2)}) async-start(f32[16,24,5120]{2,1,0:T(8,128)} %fusion.5), calls=%async_computation | async-start | bytes 15728640 | tf_op jit(solution)/shard_map/all_to_all | solution.py:68
  326.0 8.1 %copy-start = (bf16[3,20,20,1,2,288]{5,4,3,2,1,0:T(2,128)(2,1)S(1)}, bf16[3,20,20,1,2,288]{5,4,3,2,1,0:T(2,128)(2,1)}, u32[]{:S(2)}) copy-start(bf16[3,20,20,1,2,288]{5,4,3,2,1,0:T(2,128)(2,1)} %param.3) | copy-start | bytes 4147204
  326.0 27.9 %all-to-all-start.1 = ((f32[8,16,2880]{2,1,0:T(8,128)}), f32[8,16,2880]{2,1,0:T(8,128)}, u32[]{:S(2)}, u32[]{:S(2)}) async-start(f32[8,16,2880]{2,1,0:T(8,128)} %reshape.331), calls=%async_computation.1 | async-start | bytes 3014656 | tf_op jit(solution)/shard_map/all_to_all | solution.py:74

commit v2 on v1

--- a/solution.py
+++ b/solution.py
@@ -38,6 +38,15 @@
     return twiddle.reshape(STEPS_T, GRID_Z, 2 * MODES_T * MODES_Z).astype(jnp.bfloat16)
 
 
+def line_parts(kept_count, axis_length):
+    frequency = kept_modes(kept_count, axis_length)
+    positions = jnp.arange(axis_length, dtype=jnp.int32)
+    phase_index = frequency[:, None] * positions[None, :] % axis_length
+    phases = 2.0 * math.pi / axis_length * phase_index.astype(jnp.float32)
+    factor = 1.0 / math.sqrt(axis_length)
+    return factor * jnp.cos(phases), factor * jnp.sin(phases)
+
+
 def line_matrix(kept_count, axis_length):
     frequency = kept_modes(kept_count, axis_length)
     positions = jnp.arange(axis_length, dtype=jnp.int32)
@@ -52,30 +61,42 @@
 
 
 def local(plume_field, mode_weights):
-    highest = lax.Precision.HIGHEST
+    high = lax.Precision.HIGH
     samples, channels, rows_x, rows_y = plume_field.shape[:4]
     parts_x = GRID_X // rows_x
     parts_y = GRID_Y // rows_y
     groups = 2 * MODES_T
     per_group = 2 * HALF_Z
     kept_here = MODES_X // parts_y
+    lanes = rows_x * rows_y
+    pairs = samples * channels
 
     twiddle = plane_table()
-    spectrum = lax.dot_general(
-        twiddle, plume_field, (((0, 1), (4, 5)), ((), ())), preferred_element_type=jnp.float32
-    )
-    spectrum = spectrum.reshape(groups, per_group, samples * channels * rows_x * rows_y)
-    moved = lax.all_to_all(spectrum, "gx", 0, 0, tiled=False)
-    moved = moved.reshape(parts_x, 2, HALF_Z, samples, channels, rows_x, rows_y)
+    field = plume_field.reshape(pairs, lanes, STEPS_T, GRID_Z)
+    spectrum = jnp.einsum("tzn,Bxtz->Bnx", twiddle, field, preferred_element_type=jnp.float32)
+    spectrum = spectrum.reshape(pairs, groups, per_group, lanes)
+    moved = lax.all_to_all(spectrum, "gx", 1, 1, tiled=False)
 
-    first = line_matrix(MODES_X, GRID_X).reshape(2, parts_y, kept_here, 2, parts_x, rows_x)
-    after_x = jnp.einsum("sKqrip,irjbcpy->Kysqjbc", first, moved, precision=highest)
-    after_x = after_x.reshape(parts_y, rows_y, -1)
+    cosines, sines = line_parts(MODES_X, GRID_X)
+    parts = jnp.stack([cosines, sines], axis=0).reshape(2, parts_y, kept_here, parts_x, rows_x)
+    eye_y = jnp.eye(rows_y, dtype=jnp.float32)
+    kron = parts[:, :, :, None, :, :, None] * eye_y[:, None, None, :]
+    kron = jnp.transpose(kron, (4, 5, 6, 0, 1, 2, 3))
+    kron = kron.reshape(parts_x, lanes, 2, parts_y, kept_here * rows_y)
+    both = lax.dot_general(moved, kron, (((1, 3), (0, 1)), ((), ())), precision=high)
+    both = both.reshape(pairs, 2, HALF_Z, 2, parts_y, kept_here * rows_y)
+    out_re = both[:, 0, :, 0] + both[:, 1, :, 1]
+    out_im = both[:, 1, :, 0] - both[:, 0, :, 1]
+    after_x = jnp.stack([out_re, out_im], axis=0)
+    after_x = jnp.transpose(after_x, (3, 0, 4, 2, 1))
+    after_x = after_x.reshape(parts_y, 2 * kept_here * rows_y, HALF_Z * pairs)
     gathered = lax.all_to_all(after_x, "gy", 0, 0, tiled=False)
-    gathered = gathered.reshape(GRID_Y, 2, kept_here, HALF_Z, samples, channels)
+    gathered = gathered.reshape(parts_y, 2, kept_here, rows_y, HALF_Z * pairs)
 
-    second = line_matrix(MODES_Y, GRID_Y)
-    after_y = jnp.einsum("tlsy,yskjbc->kbctjl", second, gathered, precision=highest)
+    second = line_matrix(MODES_Y, GRID_Y).reshape(2, MODES_Y, 2, parts_y, rows_y)
+    after_y = lax.dot_general(second, gathered, (((2, 3, 4), (1, 0, 3)), ((), ())), precision=high)
+    after_y = after_y.reshape(2, MODES_Y, kept_here, HALF_Z, samples, channels)
+    after_y = jnp.transpose(after_y, (2, 4, 5, 0, 3, 1))
     after_y = after_y.reshape(kept_here, samples, channels, 2, HALF_Z * MODES_Y)
 
     real_part = after_y[:, :, :, None, 0]

time: 409 us -> 284 us (0.69)
  local copies, waits for them, and re-layouts: 152 us -> 79.6 us
  waiting for transfers between devices: 150 us -> 103 us
  matrix products: 69.5 us -> 46.8 us
  other arithmetic: 16.6 us -> 35.6 us
    reshape x4 -> x3, local copies, waits for them, and re-layouts: 135 us -> 15.7 us  [the longest x2 11.8 us: local(): after_x = after_x.reshape(parts_y, 2 * kept_here * rows_y, HALF_Z * pairs)]
    all_to_all x1, waiting for transfers between devices: 135 us -> 86.6 us  [local(): moved = lax.all_to_all(spectrum, 'gx', 1, 1, tiled=False)]
    mul x0 -> x2, local copies, waits for them, and re-layouts: none -> 31.8 us  [local(): kron = parts[:, :, :, None, :, :, None] * eye_y[:, None, None, :]]
    dot_general x3, matrix products: 69.5 us -> 46.8 us  [the longest x1 25.9 us: local(): lax.dot_general(moved, kron, (((1, 3), (0, 1)), ((), ())), precision=high)]
    dot_general x0 -> x2, local copies, waits for them, and re-layouts: none -> 21.5 us  [the longest x1 16.6 us: local(): lax.dot_general(second, gathered, (((2, 3, 4), (1, 0, 3)), ((), ())), pre...]
    mul x0 -> x3, other arithmetic: none -> 16.7 us  [the longest x2 16.2 us: local(): kron = parts[:, :, :, None, :, :, None] * eye_y[:, None, None, :]]
    transpose x2 -> x1, local copies, waits for them, and re-layouts: 10.8 us -> 3.93 us  [local(): after_y = jnp.transpose(after_y, (2, 4, 5, 0, 3, 1))]
  transfers between devices with their start and end apart: 2 -> 2, of which waited for: 2 -> 2; matrix products, arithmetic and copies ran while one was open for 1% -> 19% of each run, Pallas kernels for 0% -> 0%
where the time goes in v2:
time: 284 us; the launch traced here: 280 us
  waiting for transfers between devices  103 us (36%)
  local copies, waits for them, and re-layouts  79.6 us (28%)
  matrix products  46.8 us (16%)
  other arithmetic  35.6 us (13%)
  starting transfers between devices  15.6 us (5%)
    all_to_all x1, waiting for transfers between devices, local(): moved = lax.all_to_all(spectrum, 'gx', 1, 1, tiled=False)  86.6 us
    mul x2, local copies, waits for them, and re-layouts, local(): kron = parts[:, :, :, None, :, :, None] * eye_y[:, None, None, :]  31.8 us
    dot_general x1, matrix products, local(): lax.dot_general(moved, kron, (((1, 3), (0, 1)), ((), ())), precision=high)  25.9 us
    dot_general x1, local copies, waits for them, and re-layouts, local(): lax.dot_general(second, gathered, (((2, 3, 4), (1, 0, 3)), ((), ())), pre...  16.6 us
    mul x2, other arithmetic, local(): kron = parts[:, :, :, None, :, :, None] * eye_y[:, None, None, :]  16.2 us
    all_to_all x1, waiting for transfers between devices, local(): gathered = lax.all_to_all(after_x, 'gy', 0, 0, tiled=False)  16 us
    dot_general x1, matrix products, local(): jnp.einsum('tzn,Bxtz->Bnx', twiddle, field, preferred_element_type=jnp.fl...  12.1 us
    reshape x2, local copies, waits for them, and re-layouts, local(): after_x = after_x.reshape(parts_y, 2 * kept_here * rows_y, HALF_Z * pairs)  11.8 us
  transfers between devices with their start and end apart: 2, of which 2 were waited for; matrix products, arithmetic and copies ran while one was open for 19% of the time, Pallas kernels for 0%

profile of v2, /device:TPU:1, one launch (start us, length us, event | category | flops | bytes accessed | tf_op | source)
XLA Modules:
  0.0 280.4 jit_solution(1228615073364703145)
XLA Ops:
  0.1 6.7 %multiply_convert_fusion.1 = (bf16[16,128,8,2,1,12]{1,0,5,4,3,2:T(8,128)(2,1)S(1)}, bf16[16,128,8,2,1,12]{1,0,5,4,3,2:T(8,128)(2,1)S(1)}) fusion(s32[128,2,12]{0,2,1:T(8,128)S(1)} %iota_multiply_fusion, s32[16,8]{0,1:T(8,128)S(1)} %multiply_multiply_fusion), kind=kLoop, calls=%fused_computation.30 | loop fusion | flops 7077888 | bytes 1585664 | tf_op jit(solution)/shard_map/convert.2
  6.7 0.2 pad_maximum_fusion
  6.9 12.1 %fusion = f32[384,40,128,1]{2,0,3,1:T(8,128)S(1)} fusion(bf16[40,128,16,128]{3,2,1,0:T(8,128)(2,1)} %bitcast.98, bf16[16,128,384]{1,0,2:T(8,128)(2,1)S(1)} %bitcast.95), kind=kOutput, calls=%fused_computation.1 | convolution fusion | flops 8053063680 | bytes 30408704 | tf_op jit(solution)/shard_map/tzn,Bxtz->Bnx/dot_general | solution.py:76
  19.0 3.9 %copy.63 = f32[40,16,24,128]{3,2,0,1:T(8,128)} copy(f32[40,16,24,128]{3,2,1,0:T(8,128)S(1)} %bitcast.94) | data formatting | bytes 15728640 | tf_op jit(solution)/shard_map/reshape | solution.py:77
  22.9 7.6 %all-to-all-start = ((f32[40,16,24,128]{3,2,0,1:T(8,128)}), f32[40,16,24,128]{3,2,0,1:T(8,128)}, u32[]{:S(2)}, u32[]{:S(2)}) async-start(f32[40,16,24,128]{3,2,0,1:T(8,128)} %copy.63), calls=%async_computation | async-start | bytes 15728640 | tf_op jit(solution)/shard_map/all_to_all | solution.py:78
  30.5 0.5 cosine_multiply_fusion
  31.0 0.3 copy.65
  31.3 16.2 %broadcast_multiply_fusion = f32[16,8,16,2,8,3,16]{2,1,6,5,0,4,3:T(8,128)} fusion(f32[16,16]{0,1:T(8,128)S(1)} %fusion.36, f32[16,8,2,8,3]{1,4,0,3,2:T(4,128)S(1)} %copy.65), kind=kLoop, calls=%fused_computation | loop fusion | flops 1572864 | bytes 6317056 | tf_op jit(solution)/shard_map/mul | solution.py:83
  47.5 31.6 %reshape.429 = f32[16,128,2,8,48,1,1]{1,4,0,3,2,5,6:T(8,128)} reshape(f32[16,8,16,2,8,3,16]{2,1,6,5,0,4,3:T(8,128)} %broadcast_multiply_fusion) | data formatting | bytes 12582912 | tf_op jit(solution)/shard_map/mul | solution.py:83
  79.1 86.6 %all-to-all-done = f32[40,16,24,128]{3,2,0,1:T(8,128)} async-done(((f32[40,16,24,128]{3,2,0,1:T(8,128)}), f32[40,16,24,128]{3,2,0,1:T(8,128)}, u32[]{:S(2)}, u32[]{:S(2)}) %all-to-all-start) | async-done | bytes 7864352 | tf_op jit(solution)/shard_map/all_to_all | solution.py:78
  165.7 4.9 %copy.64 = f32[40,24,16,128]{3,0,2,1:T(8,128)S(1)} copy(f32[40,24,16,128]{3,1,0,2:T(8,128)} %bitcast.9) | data formatting | bytes 15728640 | tf_op jit(solution)/shard_map/dot_general | solution.py:86
  170.6 0.1 copy-done.1
  170.7 25.9 %fusion.7 = f32[40,2,12,2,8,48]{5,0,4,3,2,1:T(8,128)S(1)} fusion(f32[40,2,12,16,128,1,1]{4,0,3,6,5,2,1:T(8,128)S(1)} %bitcast.93, f32[16,128,2,8,48,1,1]{1,4,0,3,2,5,6:T(8,128)S(1)} %copy-done.1), kind=kOutput, calls=%fused_computation.11 | convolution fusion | flops 9059696640 | bytes 17104896 | tf_op jit(solution)/shard_map/dot_general | solution.py:86
  196.6 0.2 fusion.10
  196.8 0.2 fusion.12
  197.0 2.2 maximum_bitcast_fusion
  199.3 6.3 %copy.84 = f32[8,2,48,12,40]{4,3,2,1,0:T(8,128)} copy(f32[8,2,48,12,40]{2,4,0,3,1:T(8,128)} %maximum_bitcast_fusion) | data formatting | bytes 2949120 | tf_op jit(solution)/shard_map/reshape | solution.py:92
  205.5 5.5 %reshape.435 = f32[8,96,480]{2,1,0:T(8,128)} reshape(f32[8,2,48,12,40]{4,3,2,1,0:T(8,128)} %copy.84) | data formatting | bytes 2949120 | tf_op jit(solution)/shard_map/reshape | solution.py:92
  211.0 8.0 %all-to-all-start.1 = ((f32[8,96,480]{2,1,0:T(8,128)}), f32[8,96,480]{2,1,0:T(8,128)}, u32[]{:S(2)}, u32[]{:S(2)}) async-start(f32[8,96,480]{2,1,0:T(8,128)} %reshape.435), calls=%async_computation.1 | async-start | bytes 3145728 | tf_op jit(solution)/shard_map/all_to_all | solution.py:93
  219.0 0.3 sine_multiply_fusion.1
  219.4 2.5 fusion.38
  221.9 1.8 fusion.21
  223.7 16.0 %all-to-all-done.1 = f32[8,96,480]{2,1,0:T(8,128)} async-done(((f32[8,96,480]{2,1,0:T(8,128)}), f32[8,96,480]{2,1,0:T(8,128)}, u32[]{:S(2)}, u32[]{:S(2)}) %all-to-all-start.1) | async-done | bytes 1474592 | tf_op jit(solution)/shard_map/all_to_all | solution.py:93
  239.7 16.6 %reshape.436 = f32[3,12,2,20,2,8,16]{3,2,1,6,0,4,5:T(2,128)} reshape(f32[3,480,2,8,16]{1,4,0,2,3:T(8,128)} %bitcast.22) | data formatting | bytes 2949120 | tf_op jit(solution)/shard_map/dot_general | solution.py:97
  256.3 8.9 %fusion.18 = f32[3,2,20,2,12,24]{2,5,1,4,0,3:T(8,128)} fusion(f32[3,12,2,20,2,8,16]{3,2,1,6,0,4,5:T(2,128)} %reshape.436, f32[1,24,1,8,16]{1,4,3,2,0:T(8,128)S(1)} %get-tuple-element.17, f32[1,24,1,8,16]{1,4,3,2,0:T(8,128)S(1)} %get-tuple-element.16, f32[1,24,1,8,16]{1,4,3,2,0:T(8,128)S(1)} %get-tuple-element.15), kind=kOutput, calls=%fused_computation.31 | convolution fusion | flops 106205184 | bytes 1787904 | tf_op jit(solution)/shard_map/dot_general | solution.py:97
  265.2 3.9 %copy.72 = f32[3,2,20,2,12,24]{5,4,3,2,1,0:T(8,128)} copy(f32[3,2,20,2,12,24]{2,5,1,4,0,3:T(8,128)} %fusion.18) | data formatting | bytes 552960 | tf_op jit(solution)/shard_map/transpose | solution.py:99
  269.1 2.6 reshape.423
  271.7 0.3 fusion.39
  272.0 0.2 copy_bitcast_fusion.2
  272.2 7.1 %subtract_reduce_fusion = (f32[3,2,20,288]{3,1,2,0:T(2,128)S(1)}, f32[3,2,20,288]{3,1,2,0:T(2,128)S(1)}) fusion(f32[3,20,20,288]{3,2,1,0:T(8,128)S(1)} %get-tuple-element.18, f32[3,2,20,288]{3,1,2,0:T(2,128)S(1)} %get-tuple-element.20, f32[3,20,20,288]{3,2,1,0:T(8,128)} %get-tuple-element.19, f32[3,2,20,288]{3,1,2,0:T(2,128)S(1)} %get-tuple-element.21), kind=kLoop, calls=%fused_computation.10 | loop fusion | flops 5460480 | bytes 3317760 | tf_op jit(solution)/shard_map/reduce_sum | solution.py:106
  279.2 0.2 maximum_bitcast_fusion.1
  279.4 0.9 copy.77
  (12 shorter events, 0.1 us)
Async XLA Ops:
  22.9 142.8 %all-to-all-start = ((f32[40,16,24,128]{3,2,0,1:T(8,128)}), f32[40,16,24,128]{3,2,0,1:T(8,128)}, u32[]{:S(2)}, u32[]{:S(2)}) async-start(f32[40,16,24,128]{3,2,0,1:T(8,128)} %copy.63), calls=%async_computation | async-start | bytes 15728640 | tf_op jit(solution)/shard_map/all_to_all | solution.py:78
  165.7 5.0 %copy-start.1 = (f32[16,128,2,8,48,1,1]{1,4,0,3,2,5,6:T(8,128)S(1)}, f32[16,128,2,8,48,1,1]{1,4,0,3,2,5,6:T(8,128)}, u32[]{:S(2)}) copy-start(f32[16,128,2,8,48,1,1]{1,4,0,3,2,5,6:T(8,128)} %reshape.429) | copy-start | bytes 18874372
  211.0 8.3 %copy-start = (bf16[3,20,20,1,2,288]{5,4,3,2,1,0:T(2,128)(2,1)S(1)}, bf16[3,20,20,1,2,288]{5,4,3,2,1,0:T(2,128)(2,1)}, u32[]{:S(2)}) copy-start(bf16[3,20,20,1,2,288]{5,4,3,2,1,0:T(2,128)(2,1)} %param.3) | copy-start | bytes 4147204
  211.0 28.6 %all-to-all-start.1 = ((f32[8,96,480]{2,1,0:T(8,128)}), f32[8,96,480]{2,1,0:T(8,128)}, u32[]{:S(2)}, u32[]{:S(2)}) async-start(f32[8,96,480]{2,1,0:T(8,128)} %reshape.435), calls=%async_computation.1 | async-start | bytes 3145728 | tf_op jit(solution)/shard_map/all_to_all | solution.py:93

commit v3 on v2

--- a/solution.py
+++ b/solution.py
@@ -88,16 +88,20 @@
     out_re = both[:, 0, :, 0] + both[:, 1, :, 1]
     out_im = both[:, 1, :, 0] - both[:, 0, :, 1]
     after_x = jnp.stack([out_re, out_im], axis=0)
-    after_x = jnp.transpose(after_x, (3, 0, 4, 2, 1))
-    after_x = after_x.reshape(parts_y, 2 * kept_here * rows_y, HALF_Z * pairs)
+    after_x = after_x.reshape(2, pairs, HALF_Z, parts_y, kept_here, rows_y)
+    after_x = jnp.transpose(after_x, (3, 4, 0, 5, 2, 1))
+    after_x = after_x.reshape(parts_y, kept_here * 2 * rows_y, HALF_Z * pairs)
     gathered = lax.all_to_all(after_x, "gy", 0, 0, tiled=False)
-    gathered = gathered.reshape(parts_y, 2, kept_here, rows_y, HALF_Z * pairs)
+    gathered = gathered.reshape(parts_y, kept_here, 2 * rows_y, HALF_Z * pairs)
 
     second = line_matrix(MODES_Y, GRID_Y).reshape(2, MODES_Y, 2, parts_y, rows_y)
-    after_y = lax.dot_general(second, gathered, (((2, 3, 4), (1, 0, 3)), ((), ())), precision=high)
-    after_y = after_y.reshape(2, MODES_Y, kept_here, HALF_Z, samples, channels)
-    after_y = jnp.transpose(after_y, (2, 4, 5, 0, 3, 1))
+    second = jnp.transpose(second, (3, 2, 4, 0, 1)).reshape(parts_y, 2 * rows_y, 1, 2 * MODES_Y)
+    second = jnp.broadcast_to(second, (parts_y, 2 * rows_y, kept_here, 2 * MODES_Y))
+    after_y = lax.dot_general(gathered, second, (((0, 2), (0, 1)), ((1,), (2,))), precision=high)
+    after_y = after_y.reshape(kept_here, HALF_Z, samples, channels, 2, MODES_Y)
+    after_y = jnp.transpose(after_y, (0, 2, 3, 4, 1, 5))
     after_y = after_y.reshape(kept_here, samples, channels, 2, HALF_Z * MODES_Y)
+
 
     real_part = after_y[:, :, :, None, 0]
     imag_part = after_y[:, :, :, None, 1]

time: 284 us -> 270 us (0.951)
  local copies, waits for them, and re-layouts: 79.6 us -> 72 us
  matrix products: 46.8 us -> 39.9 us
    dot_general x1 -> x0, local copies, waits for them, and re-layouts: 16.6 us -> none  [local(): lax.dot_general(second, gathered, (((2, 3, 4), (1, 0, 3)), ((), ())), pre...]
    dot_general x1, matrix products: 8.89 us -> 1.97 us  [local(): lax.dot_general(gathered, second, (((0, 2), (0, 1)), ((1,), (2,))), preci...]
    transpose x1 -> x3, local copies, waits for them, and re-layouts: 3.93 us -> 10.2 us  [the longest x1 5.45 us: local(): after_x = jnp.transpose(after_x, (3, 4, 0, 5, 2, 1))]
    sub x0 -> x1, local copies, waits for them, and re-layouts: none -> 3.04 us  [local(): out_im = both[:, 1, :, 0] - both[:, 0, :, 1]]
  transfers between devices with their start and end apart: 2 -> 2, of which waited for: 2 -> 2; matrix products, arithmetic and copies ran while one was open for 19% -> 20% of each run, Pallas kernels for 0% -> 0%
where the time goes in v3:
time: 270 us; the launch traced here: 267 us
  waiting for transfers between devices  102 us (38%)
  local copies, waits for them, and re-layouts  72 us (27%)
  matrix products  39.9 us (15%)
  other arithmetic  37.3 us (14%)
  starting transfers between devices  15.6 us (6%)
    all_to_all x1, waiting for transfers between devices, local(): moved = lax.all_to_all(spectrum, 'gx', 1, 1, tiled=False)  86.7 us
    mul x2, local copies, waits for them, and re-layouts, local(): kron = parts[:, :, :, None, :, :, None] * eye_y[:, None, None, :]  31.8 us
    dot_general x1, matrix products, local(): lax.dot_general(moved, kron, (((1, 3), (0, 1)), ((), ())), precision=high)  25.8 us
    mul x2, other arithmetic, local(): kron = parts[:, :, :, None, :, :, None] * eye_y[:, None, None, :]  16.2 us
    all_to_all x1, waiting for transfers between devices, local(): gathered = lax.all_to_all(after_x, 'gy', 0, 0, tiled=False)  15.6 us
    dot_general x1, matrix products, local(): jnp.einsum('tzn,Bxtz->Bnx', twiddle, field, preferred_element_type=jnp.fl...  12.1 us
    all_to_all x1, starting transfers between devices, local(): gathered = lax.all_to_all(after_x, 'gy', 0, 0, tiled=False)  7.96 us
    all_to_all x1, starting transfers between devices, local(): moved = lax.all_to_all(spectrum, 'gx', 1, 1, tiled=False)  7.62 us
  transfers between devices with their start and end apart: 2, of which 2 were waited for; matrix products, arithmetic and copies ran while one was open for 20% of the time, Pallas kernels for 0%

profile of v3, /device:TPU:1, one launch (start us, length us, event | category | flops | bytes accessed | tf_op | source)
XLA Modules:
  0.0 267.1 jit_solution(13580642633268028038)
XLA Ops:
  0.1 6.7 %multiply_convert_fusion.1 = (bf16[16,128,8,2,1,12]{1,0,5,4,3,2:T(8,128)(2,1)S(1)}, bf16[16,128,8,2,1,12]{1,0,5,4,3,2:T(8,128)(2,1)S(1)}) fusion(s32[128,2,12]{0,2,1:T(8,128)S(1)} %iota_multiply_fusion, s32[16,8]{0,1:T(8,128)S(1)} %multiply_multiply_fusion), kind=kLoop, calls=%fused_computation.23 | loop fusion | flops 7077888 | bytes 1585664 | tf_op jit(solution)/shard_map/convert.2
  6.9 12.1 %fusion = f32[384,40,128,1]{2,0,3,1:T(8,128)S(1)} fusion(bf16[40,128,16,128]{3,2,1,0:T(8,128)(2,1)} %bitcast.75, bf16[16,128,384]{1,0,2:T(8,128)(2,1)S(1)} %bitcast.72), kind=kOutput, calls=%fused_computation.1 | convolution fusion | flops 8053063680 | bytes 30408704 | tf_op jit(solution)/shard_map/tzn,Bxtz->Bnx/dot_general | solution.py:76
  19.0 3.9 %copy.67 = f32[40,16,24,128]{3,2,0,1:T(8,128)} copy(f32[40,16,24,128]{3,2,1,0:T(8,128)S(1)} %bitcast.70) | data formatting | bytes 15728640 | tf_op jit(solution)/shard_map/reshape | solution.py:77
  22.9 7.6 %all-to-all-start = ((f32[40,16,24,128]{3,2,0,1:T(8,128)}), f32[40,16,24,128]{3,2,0,1:T(8,128)}, u32[]{:S(2)}, u32[]{:S(2)}) async-start(f32[40,16,24,128]{3,2,0,1:T(8,128)} %copy.67), calls=%async_computation | async-start | bytes 15728640 | tf_op jit(solution)/shard_map/all_to_all | solution.py:78
  30.5 0.5 cosine_multiply_fusion
  31.0 0.3 copy.69
  31.3 16.1 %broadcast_multiply_fusion = f32[16,8,16,2,8,3,16]{2,1,6,5,0,4,3:T(8,128)} fusion(f32[16,16]{0,1:T(8,128)S(1)} %fusion.22, f32[16,8,2,8,3]{1,4,0,3,2:T(4,128)S(1)} %copy.69), kind=kLoop, calls=%fused_computation | loop fusion | flops 1572864 | bytes 6317056 | tf_op jit(solution)/shard_map/mul | solution.py:83
  47.5 31.6 %reshape.440 = f32[16,128,2,8,48,1,1]{1,4,0,3,2,5,6:T(8,128)} reshape(f32[16,8,16,2,8,3,16]{2,1,6,5,0,4,3:T(8,128)} %broadcast_multiply_fusion) | data formatting | bytes 12582912 | tf_op jit(solution)/shard_map/mul | solution.py:83
  79.0 86.7 %all-to-all-done = f32[40,16,24,128]{3,2,0,1:T(8,128)} async-done(((f32[40,16,24,128]{3,2,0,1:T(8,128)}), f32[40,16,24,128]{3,2,0,1:T(8,128)}, u32[]{:S(2)}, u32[]{:S(2)}) %all-to-all-start) | async-done | bytes 7864352 | tf_op jit(solution)/shard_map/all_to_all | solution.py:78
  165.7 4.9 %copy.68 = f32[40,24,16,128]{3,0,2,1:T(8,128)S(1)} copy(f32[40,24,16,128]{3,1,0,2:T(8,128)} %bitcast.7) | data formatting | bytes 15728640 | tf_op jit(solution)/shard_map/dot_general | solution.py:86
  170.7 25.8 %fusion.4 = f32[40,2,12,2,8,48]{5,0,4,3,2,1:T(8,128)S(1)} fusion(f32[40,2,12,16,128,1,1]{4,0,3,6,5,2,1:T(8,128)S(1)} %bitcast.69, f32[16,128,2,8,48,1,1]{1,4,0,3,2,5,6:T(8,128)S(1)} %copy-done.1), kind=kOutput, calls=%fused_computation.8 | convolution fusion | flops 9059696640 | bytes 17104896 | tf_op jit(solution)/shard_map/dot_general | solution.py:86
  196.6 2.3 slice_add_fusion
  198.9 2.0 copy.70
  200.9 3.0 %copy.71 = f32[40,1,12,1,8,48]{0,5,4,2,3,1:T(8,128)} copy(f32[40,1,12,1,8,48]{5,0,4,3,2,1:T(8,128)} %get-tuple-element.8) | data formatting | bytes 1474560 | tf_op jit(solution)/shard_map/sub | solution.py:89
  204.0 2.0 maximum_bitcast_fusion
  206.0 5.4 %copy.72 = f32[8,3,2,16,12,40]{5,4,3,2,1,0:T(8,128)} copy(f32[8,3,2,16,12,40]{5,3,1,0,4,2:T(8,128)S(1)} %maximum_bitcast_fusion) | data formatting | bytes 2949120 | tf_op jit(solution)/shard_map/transpose | solution.py:92
  211.4 5.5 %reshape.431 = f32[8,96,480]{2,1,0:T(8,128)} reshape(f32[8,3,2,16,12,40]{5,4,3,2,1,0:T(8,128)} %copy.72) | data formatting | bytes 2949120 | tf_op jit(solution)/shard_map/reshape | solution.py:93
  216.9 8.0 %all-to-all-start.1 = ((f32[8,96,480]{2,1,0:T(8,128)}), f32[8,96,480]{2,1,0:T(8,128)}, u32[]{:S(2)}, u32[]{:S(2)}) async-start(f32[8,96,480]{2,1,0:T(8,128)} %reshape.431), calls=%async_computation.1 | async-start | bytes 3145728 | tf_op jit(solution)/shard_map/all_to_all | solution.py:94
  224.9 0.3 sine_multiply_fusion.1
  225.3 0.2 copy.73
  225.5 0.2 broadcast_in_dim.6
  225.7 2.5 fusion.23
  228.2 1.8 fusion.12
  230.0 15.6 %all-to-all-done.1 = f32[8,96,480]{2,1,0:T(8,128)} async-done(((f32[8,96,480]{2,1,0:T(8,128)}), f32[8,96,480]{2,1,0:T(8,128)}, u32[]{:S(2)}, u32[]{:S(2)}) %all-to-all-start.1) | async-done | bytes 1474592 | tf_op jit(solution)/shard_map/all_to_all | solution.py:94
  245.6 2.0 convolution_bitcast_fusion
  247.6 3.8 %reshape.433 = f32[3,12,2,20,2,24]{3,2,1,5,4,0:T(2,128)} reshape(f32[3,480,48]{1,2,0:T(8,128)S(1)} %convolution_bitcast_fusion) | data formatting | bytes 552960 | tf_op jit(solution)/shard_map/reshape | solution.py:101
  251.4 4.5 %copy.74 = f32[3,2,20,2,12,24]{5,4,3,2,1,0:T(8,128)} copy(f32[3,2,20,2,12,24]{2,1,4,5,3,0:T(2,128)} %bitcast.71) | data formatting | bytes 552960 | tf_op jit(solution)/shard_map/transpose | solution.py:102
  255.9 2.6 reshape.434
  258.5 0.3 fusion.24
  258.8 0.2 copy_bitcast_fusion.2
  259.0 7.1 %subtract_reduce_fusion = (f32[3,2,20,288]{3,1,2,0:T(2,128)S(1)}, f32[3,2,20,288]{3,1,2,0:T(2,128)S(1)}) fusion(f32[3,20,20,288]{3,2,1,0:T(8,128)S(1)} %get-tuple-element.20, f32[3,2,20,288]{3,1,2,0:T(2,128)S(1)} %get-tuple-element.22, f32[3,20,20,288]{3,2,1,0:T(8,128)} %get-tuple-element.21, f32[3,2,20,288]{3,1,2,0:T(2,128)S(1)} %get-tuple-element.23), kind=kLoop, calls=%fused_computation.7 | loop fusion | flops 5460480 | bytes 3317760 | tf_op jit(solution)/shard_map/reduce_sum | solution.py:110
  266.2 0.9 copy.79
  (16 shorter events, 0.6 us)
Async XLA Ops:
  22.9 142.8 %all-to-all-start = ((f32[40,16,24,128]{3,2,0,1:T(8,128)}), f32[40,16,24,128]{3,2,0,1:T(8,128)}, u32[]{:S(2)}, u32[]{:S(2)}) async-start(f32[40,16,24,128]{3,2,0,1:T(8,128)} %copy.67), calls=%async_computation | async-start | bytes 15728640 | tf_op jit(solution)/shard_map/all_to_all | solution.py:78
  165.7 5.0 %copy-start.1 = (f32[16,128,2,8,48,1,1]{1,4,0,3,2,5,6:T(8,128)S(1)}, f32[16,128,2,8,48,1,1]{1,4,0,3,2,5,6:T(8,128)}, u32[]{:S(2)}) copy-start(f32[16,128,2,8,48,1,1]{1,4,0,3,2,5,6:T(8,128)} %reshape.440) | copy-start | bytes 18874372
  216.9 8.7 %copy-start = (bf16[3,20,20,1,2,288]{5,4,3,2,1,0:T(2,128)(2,1)S(1)}, bf16[3,20,20,1,2,288]{5,4,3,2,1,0:T(2,128)(2,1)}, u32[]{:S(2)}) copy-start(bf16[3,20,20,1,2,288]{5,4,3,2,1,0:T(2,128)(2,1)} %param.3) | copy-start | bytes 4147204
  216.9 28.7 %all-to-all-start.1 = ((f32[8,96,480]{2,1,0:T(8,128)}), f32[8,96,480]{2,1,0:T(8,128)}, u32[]{:S(2)}, u32[]{:S(2)}) async-start(f32[8,96,480]{2,1,0:T(8,128)} %reshape.431), calls=%async_computation.1 | async-start | bytes 3145728 | tf_op jit(solution)/shard_map/all_to_all | solution.py:94
